TPU v7x, 512 devices: a whole 4x8x8 slice. The times are simulated.
512 devices in a mesh: context: 64 (over y, z), channel: 8 (over x, core).
Axes of the slice: x: 4, y: 8, z: 8, core: 2. Of those that a mesh axis runs over, the one named last changes fastest.
Arguments:
- inputs: bfloat16 [512, 32768], P('channel', 'context'), may hold values from -6 to 6
- grad_out: bfloat16 [512, 32768], P('channel', 'context'), may hold values from -36 to 36
- decay_rates: float32 [64, 16], replicated, as said below
- residues: float32 [64, 16], replicated, may hold values from -1.5 to 1.5
Outputs:
- grad_in: bfloat16 [512, 32768], P('channel', 'context')
- grad_residue: float32 [64, 16], replicated
- grad_log_rate: float32 [64, 16], replicated
Inputs may be any that keep to these rules, and one draw needn't show every extreme that they name: `decay_rates`: every rate lies between 0.3 / 32768 and 1 / 15.
All inputs are finite; a program needn't handle non-finite values.
Results may differ from a plain program's by a relative error of at most 0.001.
Values may be sent and summed in bfloat16 or wider, within the bound.
No kernel may reach another device: no remote copies, remote signals or barrier semaphores. Data moves between devices by JAX's collectives and lax.ppermute only.
A program may use at most 64 MiB of HBM per device.

v0:
```python
import math
import jax
import jax.numpy as jnp
from jax import lax
from jax.sharding import PartitionSpec as P

precise_setting = lax.Precision.HIGHEST


def forward_combine(earlier, later):
    decay_one, cross_one, state_one, slope_one = earlier
    decay_two, cross_two, state_two, second_slope = later
    return (
        decay_two * decay_one,
        decay_two * cross_one + cross_two * decay_one,
        decay_two * state_one + state_two,
        decay_two * slope_one + cross_two * state_one + second_slope,
    )


def backward_combine(earlier, later):
    decay_far, total_far = earlier
    decay_near, total_near = later
    return (decay_far * decay_near, total_near + decay_near * total_far)


def within_blocks(x_rows, g_rows, decay_rates, block_len):
    chan_count, pole_count = decay_rates.shape
    quarter = pole_count // 4
    offset = jnp.arange(block_len, dtype=jnp.float32)
    centre = float(block_len // 2)
    upper_ones = (offset[:, None] <= offset[None, :]).astype(jnp.float32)
    grouped = decay_rates.reshape(chan_count, 4, quarter).transpose(1, 0, 2)

    def one_group(rate_part):
        rate_col = rate_part[:, :, None]
        x_scaled = x_rows[:, None, :, :] * jnp.exp(-rate_col * (centre - offset))[:, :, None, :]
        g_scaled = g_rows[:, None, :, :] * jnp.exp(-rate_col * (offset - centre))[:, :, None, :]
        stacked = jnp.stack([x_scaled, x_scaled * offset], axis=2)
        running = jnp.einsum("nqsbv,vu->nqsbu", stacked, upper_ones, precision=precise_setting)
        first_part = jnp.sum(g_scaled * running[:, :, 0], axis=(2, 3))
        second_part = jnp.sum(
            g_scaled * (offset * running[:, :, 0] - running[:, :, 1]), axis=(2, 3)
        )
        return (first_part, second_part)

    first_all, second_all = lax.map(one_group, grouped)
    return (
        first_all.transpose(1, 0, 2).reshape(chan_count, pole_count),
        second_all.transpose(1, 0, 2).reshape(chan_count, pole_count),
    )


def prepare(inputs, grad_out, decay_rates, block_len):
    chan_count, length = inputs.shape
    blocks = length // block_len
    x_rows = inputs.astype(jnp.float32).reshape(chan_count, blocks, block_len)
    g_rows = grad_out.astype(jnp.float32).reshape(chan_count, blocks, block_len)
    offset = jnp.arange(block_len, dtype=jnp.float32)
    tail_pos = block_len - 1.0 - offset
    rate_col = decay_rates[:, :, None]
    tail_pow = jnp.exp(-rate_col * tail_pos)
    next_pow = jnp.exp(-rate_col * (offset + 1.0))
    x_weights = jnp.stack([tail_pow, tail_pos * tail_pow], axis=2)
    g_weights = jnp.stack(
        [next_pow, (offset + 1.0) * next_pow, jnp.exp(-rate_col * offset)], axis=2
    )
    x_ends = jnp.einsum("nbj,nksj->nksb", x_rows, x_weights, precision=precise_setting)
    g_ends = jnp.einsum("nbj,nksj->nksb", g_rows, g_weights, precision=precise_setting)
    block_decay = jnp.broadcast_to(
        jnp.exp(-decay_rates * block_len)[:, :, None], x_ends[:, :, 0].shape
    )
    forward = lax.associative_scan(
        forward_combine,
        (block_decay, block_len * block_decay, x_ends[:, :, 0], x_ends[:, :, 1]),
        axis=2,
    )
    backward = lax.associative_scan(
        backward_combine, (block_decay, g_ends[:, :, 2]), axis=2, reverse=True
    )
    first_in, second_in = within_blocks(x_rows, g_rows, decay_rates, block_len)
    return (g_rows, forward, backward, g_ends, first_in, second_in)


def complete(prepared, start_state, start_slope, end_adjoint, decay_rates, residues, block_len):
    g_rows, forward, backward, g_ends, first_in, second_in = prepared
    chan_count, blocks, _ = g_rows.shape
    unit_col = jnp.ones(decay_rates.shape + (1,), jnp.float32)
    zero_col = jnp.zeros_like(unit_col)
    lead_decay = jnp.concatenate([unit_col, forward[0][:, :, :-1]], axis=2)
    lead_cross = jnp.concatenate([zero_col, forward[1][:, :, :-1]], axis=2)
    lead_state = jnp.concatenate([zero_col, forward[2][:, :, :-1]], axis=2)
    lead_slope = jnp.concatenate([zero_col, forward[3][:, :, :-1]], axis=2)
    enter_state = lead_decay * start_state[:, :, None] + lead_state
    enter_slope = (
        lead_decay * start_slope[:, :, None] + lead_cross * start_state[:, :, None] + lead_slope
    )
    first_sum = first_in + jnp.sum(enter_state * g_ends[:, :, 0], axis=2)
    second_sum = second_in + jnp.sum(
        enter_slope * g_ends[:, :, 0] + enter_state * g_ends[:, :, 1], axis=2
    )
    decay_step = jnp.exp(-decay_rates)
    gain_pole = jnp.sqrt(-jnp.expm1(-2.0 * decay_rates))
    residue_gradient = gain_pole * first_sum
    log_grad = (
        residues
        * decay_rates
        * (decay_step * decay_step / gain_pole * first_sum - gain_pole * second_sum)
    )
    weighted = residues * gain_pole
    trail_decay = jnp.concatenate([backward[0][:, :, 1:], unit_col], axis=2)
    trail_total = jnp.concatenate([backward[1][:, :, 1:], zero_col], axis=2)
    incoming = (trail_total + trail_decay * end_adjoint[:, :, None]) * weighted[:, :, None]
    offset = jnp.arange(block_len, dtype=jnp.float32)
    centre = float(block_len // 2)
    rate_col = decay_rates[:, :, None]
    carried = jnp.einsum(
        "nkb,nkj->nbj",
        incoming,
        jnp.exp(-rate_col * (block_len - offset)),
        precision=precise_setting,
    )
    row_multiplier = weighted[:, :, None] * jnp.exp(-rate_col * (offset - centre))
    column_multiplier = jnp.exp(rate_col * (offset - centre))
    lower_mask = offset[:, None] >= offset[None, :]
    toeplitz = jnp.where(
        lower_mask[None],
        jnp.einsum("acr,acq->arq", row_multiplier, column_multiplier, precision=precise_setting),
        0.0,
    )
    local_part = jnp.einsum("nbu,nuv->nbv", g_rows, toeplitz, precision=precise_setting)
    grad_in = (local_part + carried).reshape(chan_count, blocks * block_len).astype(jnp.bfloat16)
    return (grad_in, residue_gradient, log_grad)


def body(inputs, grad_out, decay_rates, residues):
    chan_count, token_count = inputs.shape
    context_size = lax.axis_size("context")
    seq_total = token_count * context_size
    group_size = lax.axis_size("channel")
    pole_count = decay_rates.shape[1]
    zero_pair = jnp.zeros_like(decay_rates)
    share = chan_count // context_size
    moved_inputs, moved_grads = (
        lax.all_to_all(inputs, "context", split_axis=0, concat_axis=1, tiled=True),
        lax.all_to_all(grad_out, "context", split_axis=0, concat_axis=1, tiled=True),
    )
    first_row = lax.axis_index("context") * share
    my_rates = lax.dynamic_slice_in_dim(decay_rates, first_row, share, 0)
    my_residues = lax.dynamic_slice_in_dim(residues, first_row, share, 0)
    block_len = math.gcd(128, seq_total)
    prepared = prepare(moved_inputs, moved_grads, my_rates, block_len)
    zero_state = jnp.zeros((share, pole_count), jnp.float32)
    grad_part, res_part, log_part = complete(
        prepared, zero_state, zero_state, zero_state, my_rates, my_residues, block_len
    )
    grad_in = lax.all_to_all(grad_part, "context", split_axis=1, concat_axis=0, tiled=True)
    res_local = lax.dynamic_update_slice_in_dim(zero_pair, res_part, first_row, 0)
    log_local = lax.dynamic_update_slice_in_dim(zero_pair, log_part, first_row, 0)
    res_total, log_total = lax.psum((res_local, log_local), ("context", "channel"))
    norm_scale = 1.0 / math.sqrt(seq_total * group_size)
    return (grad_in, res_total * norm_scale, log_total * norm_scale)


def solution(mesh):
    return jax.shard_map(
        body,
        mesh=mesh,
        in_specs=(P("channel", "context"), P("channel", "context"), P(), P()),
        out_specs=(P("channel", "context"), P(), P()),
        check_vma=False,
    )
```

profile of v0, /device:TPU:1, one launch (start us, length us, event | category | flops | bytes accessed | tf_op | source)
XLA Modules:
  0.0 199.6 jit_solution(9558295038052606538)
XLA Ops:
  1.1 1.5 reduce.24
  2.6 0.6 reshape.1135
  3.3 17.3 %all-to-all-start.2 = ((bf16[64,2,256]{2,1,0:T(2,128)(2,1)}), bf16[64,2,256]{2,1,0:T(2,128)(2,1)S(1)}, u32[]{:S(2)}, u32[]{:S(2)}) async-start(bf16[64,2,256]{2,1,0:T(2,128)(2,1)} %reshape.1135), calls=%async_computation.2 | async-start | bytes 131072 | tf_op jit(solution)/shard_map/all_to_all | solution.py:145
  20.6 0.7 copy-done.1
  22.4 0.7 reduce.25
  23.1 0.6 reshape.1131
  23.7 7.9 %all-to-all-done.2 = bf16[64,2,256]{2,1,0:T(2,128)(2,1)S(1)} async-done(((bf16[64,2,256]{2,1,0:T(2,128)(2,1)}), bf16[64,2,256]{2,1,0:T(2,128)(2,1)S(1)}, u32[]{:S(2)}, u32[]{:S(2)}) %all-to-all-start.2) | async-done | bytes 65568 | tf_op jit(solution)/shard_map/all_to_all | solution.py:145
  31.7 4.8 %all-to-all-start = ((bf16[64,2,256]{2,1,0:T(2,128)(2,1)}), bf16[64,2,256]{2,1,0:T(2,128)(2,1)S(1)}, u32[]{:S(2)}, u32[]{:S(2)}) async-start(bf16[64,2,256]{2,1,0:T(2,128)(2,1)} %reshape.1131), calls=%async_computation | async-start | bytes 131072 | tf_op jit(solution)/shard_map/all_to_all | solution.py:146
  43.7 3.7 %all-to-all-done = bf16[64,2,256]{2,1,0:T(2,128)(2,1)S(1)} async-done(((bf16[64,2,256]{2,1,0:T(2,128)(2,1)}), bf16[64,2,256]{2,1,0:T(2,128)(2,1)S(1)}, u32[]{:S(2)}, u32[]{:S(2)}) %all-to-all-start) | async-done | bytes 65568 | tf_op jit(solution)/shard_map/all_to_all | solution.py:146
  68.6 6.0 %while.16 = (s32[]{:T(128)}, f32[4,1,4]{2,1,0:T(1,128)S(1)}, f32[4,1,4]{2,1,0:T(1,128)S(1)}, f32[1,32768]{1,0:T(1,128)S(1)}, f32[4,1,4]{2,1,0:T(1,128)S(1)}, /*index=5*/f32[1,32768]{1,0:T(1,128)S(1)}, s32[]{:T(128)}) while((s32[]{:T(128)}, f32[4,1,4]{2,1,0:T(1,128)S(1)}, f32[4,1,4]{2,1,0:T(1,128)S(1)}, ...), condition=%wide.region_3.4_spmd.clone.clone, body=%wide.region_0.3_spmd.clone.clone.sunk | while | flops 404129024 | bytes 4468909 | solution.py:47
  69.0 1.0 convolution_bitcast_fusion.5
  70.4 1.0 convolution_bitcast_fusion.5
  71.9 1.0 convolution_bitcast_fusion.5
  73.3 1.0 convolution_bitcast_fusion.5
  75.1 0.7 reduce.22
  75.8 0.7 reduce.21
  80.1 96.9 %all-reduce.102 = (f32[64,16]{0,1:T(8,128)S(1)}, f32[64,16]{0,1:T(8,128)S(1)}) all-reduce(f32[64,16]{0,1:T(8,128)S(1)} %dynamic_update_slice.19, f32[64,16]{0,1:T(8,128)S(1)} %dynamic_update_slice.20), channel_id=1, replica_groups=mesh['context'=64,'channel'=8] {'context','channel'}, use_global_device_ids=true, to_apply=%region_5.6 | all-reduce | flops 2048 | bytes 16384 | tf_op jit(solution)/shard_map/psum | solution.py:160
  177.0 0.6 broadcast_multiply_fusion.3
  178.8 1.0 reduce.26
  179.8 0.6 reshape.1133
  180.5 7.2 %all-to-all-start.1 = ((bf16[64,2,256]{2,1,0:T(2,128)(2,1)}), bf16[64,2,256]{2,1,0:T(2,128)(2,1)S(1)}, u32[]{:S(2)}, u32[]{:S(2)}) async-start(bf16[64,2,256]{2,1,0:T(2,128)(2,1)} %reshape.1133), calls=%async_computation.1 | async-start | bytes 131072 | tf_op jit(solution)/shard_map/all_to_all | solution.py:157
  187.7 0.6 broadcast_multiply_fusion.2
  188.3 10.5 %all-to-all-done.1 = bf16[64,2,256]{2,1,0:T(2,128)(2,1)S(1)} async-done(((bf16[64,2,256]{2,1,0:T(2,128)(2,1)}), bf16[64,2,256]{2,1,0:T(2,128)(2,1)S(1)}, u32[]{:S(2)}, u32[]{:S(2)}) %all-to-all-start.1) | async-done | bytes 65568 | tf_op jit(solution)/shard_map/all_to_all | solution.py:157
  198.9 0.6 copy.204
  (375 shorter events, 36.1 us)
Async XLA Ops:
  3.3 17.3 %copy-start.2 = (f32[64,16]{0,1:T(8,128)S(1)}, f32[64,16]{0,1:T(8,128)}, u32[]{:S(2)}) copy-start(f32[64,16]{0,1:T(8,128)} %param.9) | copy-start | bytes 12292
  3.3 28.4 %all-to-all-start.2 = ((bf16[64,2,256]{2,1,0:T(2,128)(2,1)}), bf16[64,2,256]{2,1,0:T(2,128)(2,1)S(1)}, u32[]{:S(2)}, u32[]{:S(2)}) async-start(bf16[64,2,256]{2,1,0:T(2,128)(2,1)} %reshape.1135), calls=%async_computation.2 | async-start | bytes 131072 | tf_op jit(solution)/shard_map/all_to_all | solution.py:145
  20.6 0.7 copy-start.1
  21.6 0.8 copy-start
  31.7 15.7 %all-to-all-start = ((bf16[64,2,256]{2,1,0:T(2,128)(2,1)}), bf16[64,2,256]{2,1,0:T(2,128)(2,1)S(1)}, u32[]{:S(2)}, u32[]{:S(2)}) async-start(bf16[64,2,256]{2,1,0:T(2,128)(2,1)} %reshape.1131), calls=%async_computation | async-start | bytes 131072 | tf_op jit(solution)/shard_map/all_to_all | solution.py:146
  180.5 18.4 %all-to-all-start.1 = ((bf16[64,2,256]{2,1,0:T(2,128)(2,1)}), bf16[64,2,256]{2,1,0:T(2,128)(2,1)S(1)}, u32[]{:S(2)}, u32[]{:S(2)}) async-start(bf16[64,2,256]{2,1,0:T(2,128)(2,1)} %reshape.1133), calls=%async_computation.1 | async-start | bytes 131072 | tf_op jit(solution)/shard_map/all_to_all | solution.py:157
where the time goes:
time: 200 us
  blocking collectives  96.9 us (48%)
  local copies, waits for them, and re-layouts  29.6 us (15%)
  starting transfers between devices  29.3 us (15%)
  waiting for transfers between devices  22.1 us (11%)
  other arithmetic  14.1 us (7%)
  matrix products  5.37 us (3%)
    psum x1, blocking collectives, body(): lax.psum((res_local, log_local), ('context', 'channel'))  96.9 us
    all_to_all x1, starting transfers between devices, body(): lax.all_to_all(inputs, 'context', split_axis=0, concat_axis=1, tiled=True)  17.3 us
    all_to_all x1, waiting for transfers between devices, body(): lax.all_to_all(grad_part, 'context', split_axis=1, concat_axis=0, tiled=T...  10.5 us
    all_to_all x1, waiting for transfers between devices, body(): lax.all_to_all(inputs, 'context', split_axis=0, concat_axis=1, tiled=True)  7.95 us
    all_to_all x1, starting transfers between devices, body(): lax.all_to_all(grad_part, 'context', split_axis=1, concat_axis=0, tiled=T...  7.24 us
    unnamed x26, local copies, waits for them, and re-layouts  6.29 us
    slice x43, local copies, waits for them, and re-layouts, prepare(): lax.associative_scan(forward_combine, (block_decay, block_len * block_dec...  6.06 us
    slice x46, local copies, waits for them, and re-layouts, prepare(): lax.associative_scan(backward_combine, (block_decay, g_ends[:, :, 2]), ax...  5.62 us
  transfers between devices with their start and end apart: 3, of which 3 were waited for; matrix products, arithmetic and copies ran while one was open for 5% of the time, Pallas kernels for 0%

commit v1 on v0

--- a/solution.py
+++ b/solution.py
@@ -5,6 +5,12 @@
 from jax.sharding import PartitionSpec as P
 
 precise_setting = lax.Precision.HIGHEST
+
+
+def resolve_bench(u_in, lane_axis, comm_axis):
+    for b in (lane_axis, comm_axis):
+        u_in = lax.psum(u_in, b)
+    return u_in
 
 
 def forward_combine(earlier, later):
@@ -157,7 +163,9 @@
     grad_in = lax.all_to_all(grad_part, "context", split_axis=1, concat_axis=0, tiled=True)
     res_local = lax.dynamic_update_slice_in_dim(zero_pair, res_part, first_row, 0)
     log_local = lax.dynamic_update_slice_in_dim(zero_pair, log_part, first_row, 0)
-    res_total, log_total = lax.psum((res_local, log_local), ("context", "channel"))
+    res_total, log_total = resolve_bench(
+        (res_local, log_local), lane_axis="context", comm_axis="channel"
+    )
     norm_scale = 1.0 / math.sqrt(seq_total * group_size)
     return (grad_in, res_total * norm_scale, log_total * norm_scale)
 

time: 200 us -> 401 us (2.00)
  blocking collectives: 96.9 us -> 298 us
    psum x1 -> x2, blocking collectives: 96.9 us -> 298 us  [resolve_bench(): u_in = lax.psum(u_in, b)]
  transfers between devices with their start and end apart: 3 -> 3, of which waited for: 3 -> 3; matrix products, arithmetic and copies ran while one was open for 5% -> 3% of each run, Pallas kernels for 0% -> 0%
where the time goes in v1:
time: 401 us; the launch traced here: 398 us
  blocking collectives  298 us (74%)
  local copies, waits for them, and re-layouts  29.6 us (7%)
  starting transfers between devices  26.9 us (7%)
  waiting for transfers between devices  22.1 us (6%)
  other arithmetic  14.1 us (4%)
  matrix products  5.37 us (1%)
    psum x2, blocking collectives, resolve_bench(): u_in = lax.psum(u_in, b)  298 us
    all_to_all x1, starting transfers between devices, body(): lax.all_to_all(inputs, 'context', split_axis=0, concat_axis=1, tiled=True)  17.3 us
    all_to_all x1, waiting for transfers between devices, body(): lax.all_to_all(grad_part, 'context', split_axis=1, concat_axis=0, tiled=T...  10.5 us
  transfers between devices with their start and end apart: 3, of which 3 were waited for; matrix products, arithmetic and copies ran while one was open for 3% of the time, Pallas kernels for 0%

profile of v1, /device:TPU:1, one launch (start us, length us, event | category | flops | bytes accessed | tf_op | source)
XLA Modules:
  0.0 398.1 jit_solution(1085533768989655288)
XLA Ops:
  1.1 1.5 reduce.24
  2.6 0.6 reshape.1135
  3.3 17.3 %all-to-all-start.2 = ((bf16[64,2,256]{2,1,0:T(2,128)(2,1)}), bf16[64,2,256]{2,1,0:T(2,128)(2,1)S(1)}, u32[]{:S(2)}, u32[]{:S(2)}) async-start(bf16[64,2,256]{2,1,0:T(2,128)(2,1)} %reshape.1135), calls=%async_computation.2 | async-start | bytes 131072 | tf_op jit(solution)/shard_map/all_to_all | solution.py:151
  20.6 0.7 copy-done.1
  22.4 0.7 reduce.25
  23.1 0.6 reshape.1131
  23.7 8.0 %all-to-all-done.2 = bf16[64,2,256]{2,1,0:T(2,128)(2,1)S(1)} async-done(((bf16[64,2,256]{2,1,0:T(2,128)(2,1)}), bf16[64,2,256]{2,1,0:T(2,128)(2,1)S(1)}, u32[]{:S(2)}, u32[]{:S(2)}) %all-to-all-start.2) | async-done | bytes 65568 | tf_op jit(solution)/shard_map/all_to_all | solution.py:151
  31.7 4.8 %all-to-all-start = ((bf16[64,2,256]{2,1,0:T(2,128)(2,1)}), bf16[64,2,256]{2,1,0:T(2,128)(2,1)S(1)}, u32[]{:S(2)}, u32[]{:S(2)}) async-start(bf16[64,2,256]{2,1,0:T(2,128)(2,1)} %reshape.1131), calls=%async_computation | async-start | bytes 131072 | tf_op jit(solution)/shard_map/all_to_all | solution.py:152
  43.7 3.7 all-to-all-done
  68.5 6.0 %while.16 = (s32[]{:T(128)}, f32[4,1,4]{2,1,0:T(1,128)S(1)}, f32[4,1,4]{2,1,0:T(1,128)S(1)}, f32[1,32768]{1,0:T(1,128)S(1)}, f32[4,1,4]{2,1,0:T(1,128)S(1)}, /*index=5*/f32[1,32768]{1,0:T(1,128)S(1)}, s32[]{:T(128)}) while((s32[]{:T(128)}, f32[4,1,4]{2,1,0:T(1,128)S(1)}, f32[4,1,4]{2,1,0:T(1,128)S(1)}, ...), condition=%wide.region_3.4_spmd.clone.clone, body=%wide.region_0.3_spmd.clone.clone.sunk | while | flops 404129024 | bytes 4468909 | solution.py:53
  69.0 1.0 convolution_bitcast_fusion.5
  70.4 1.0 convolution_bitcast_fusion.5
  71.8 1.0 convolution_bitcast_fusion.5
  73.3 1.0 convolution_bitcast_fusion.5
  75.0 0.7 reduce.22
  75.8 0.7 reduce.21
  80.1 220.3 %all-reduce.102 = (f32[64,16]{0,1:T(8,128)S(1)}, f32[64,16]{0,1:T(8,128)S(1)}) all-reduce(f32[64,16]{0,1:T(8,128)S(1)} %dynamic_update_slice.19, f32[64,16]{0,1:T(8,128)S(1)} %dynamic_update_slice.20), channel_id=1, replica_groups=mesh['context'=64,'channel'=8] {'context'}, use_global_device_ids=true, to_apply=%region_5.6 | all-reduce | flops 2048 | bytes 16384 | tf_op jit(solution)/shard_map/psum | solution.py:12
  300.4 77.6 %all-reduce.103 = (f32[64,16]{0,1:T(8,128)S(1)}, f32[64,16]{0,1:T(8,128)S(1)}) all-reduce(f32[64,16]{0,1:T(8,128)S(1)} %get-tuple-element.205, f32[64,16]{0,1:T(8,128)S(1)} %get-tuple-element.206), channel_id=1, replica_groups=mesh['context'=64,'channel'=8] {'channel'}, use_global_device_ids=true, to_apply=%region_6.7 | all-reduce | flops 2048 | bytes 16384 | tf_op jit(solution)/shard_map/psum | solution.py:12
  379.8 1.0 reduce.26
  380.8 0.6 reshape.1133
  381.4 4.9 %all-to-all-start.1 = ((bf16[64,2,256]{2,1,0:T(2,128)(2,1)}), bf16[64,2,256]{2,1,0:T(2,128)(2,1)S(1)}, u32[]{:S(2)}, u32[]{:S(2)}) async-start(bf16[64,2,256]{2,1,0:T(2,128)(2,1)} %reshape.1133), calls=%async_computation.1 | async-start | bytes 131072 | tf_op jit(solution)/shard_map/all_to_all | solution.py:163
  386.3 0.6 broadcast_multiply_fusion.2
  386.9 10.5 %all-to-all-done.1 = bf16[64,2,256]{2,1,0:T(2,128)(2,1)S(1)} async-done(((bf16[64,2,256]{2,1,0:T(2,128)(2,1)}), bf16[64,2,256]{2,1,0:T(2,128)(2,1)S(1)}, u32[]{:S(2)}, u32[]{:S(2)}) %all-to-all-start.1) | async-done | bytes 65568 | tf_op jit(solution)/shard_map/all_to_all | solution.py:163
  397.5 0.6 copy.204
  (376 shorter events, 36.7 us)
Async XLA Ops:
  3.3 17.3 %copy-start.2 = (f32[64,16]{0,1:T(8,128)S(1)}, f32[64,16]{0,1:T(8,128)}, u32[]{:S(2)}) copy-start(f32[64,16]{0,1:T(8,128)} %param.9) | copy-start | bytes 12292
  3.3 28.4 %all-to-all-start.2 = ((bf16[64,2,256]{2,1,0:T(2,128)(2,1)}), bf16[64,2,256]{2,1,0:T(2,128)(2,1)S(1)}, u32[]{:S(2)}, u32[]{:S(2)}) async-start(bf16[64,2,256]{2,1,0:T(2,128)(2,1)} %reshape.1135), calls=%async_computation.2 | async-start | bytes 131072 | tf_op jit(solution)/shard_map/all_to_all | solution.py:151
  20.6 0.7 copy-start.1
  21.6 0.8 copy-start
  31.7 15.7 %all-to-all-start = ((bf16[64,2,256]{2,1,0:T(2,128)(2,1)}), bf16[64,2,256]{2,1,0:T(2,128)(2,1)S(1)}, u32[]{:S(2)}, u32[]{:S(2)}) async-start(bf16[64,2,256]{2,1,0:T(2,128)(2,1)} %reshape.1131), calls=%async_computation | async-start | bytes 131072 | tf_op jit(solution)/shard_map/all_to_all | solution.py:152
  381.4 16.0 %all-to-all-start.1 = ((bf16[64,2,256]{2,1,0:T(2,128)(2,1)}), bf16[64,2,256]{2,1,0:T(2,128)(2,1)S(1)}, u32[]{:S(2)}, u32[]{:S(2)}) async-start(bf16[64,2,256]{2,1,0:T(2,128)(2,1)} %reshape.1133), calls=%async_computation.1 | async-start | bytes 131072 | tf_op jit(solution)/shard_map/all_to_all | solution.py:163
